TPU v7x, 32 devices: a whole 2x2x4 slice. The times are simulated.
32 devices in a mesh: dp: 16 (over z, x, core), rep: 2 (over y).
Axes of the slice: x: 2, y: 2, z: 4, core: 2. Of those that a mesh axis runs over, the one named last changes fastest.
Arguments:
- grad_out: bfloat16 [12288, 2048], P('dp', 'rep'), may hold values from -6 to 6
- pre_act: bfloat16 [12288, 3072], P('dp', 'rep'), may hold values from -6 to 6
- up_weight: bfloat16 [3072, 2048], P('rep'), may hold values from -0.125 to 0.125
- down_weight: bfloat16 [2048, 3072], P(None, 'rep'), may hold values from -0.109375 to 0.109375
- slot_counts: int32 [16], P('dp'), may hold values from 384 to 768, as said below
Outputs:
- input_grad: bfloat16 [12288, 2048], P('dp')
- down_grad: float32 [2048, 3072], P('dp', 'rep')
Inputs may be any that keep to these rules, and one draw needn't show every extreme that they name: Row i * 768 + j is live exactly when j < slot_counts[i]; some index has all 768 slots live and some index exactly 384.
All inputs are finite; a program needn't handle non-finite values.
Results may differ from a plain program's by a relative error of at most 0.0049.
Values may be sent and summed in bfloat16 or wider, within the bound.
A program may use at most 128 MiB of HBM per device.

v0:
```python
import functools

import jax
import jax.numpy as jnp
from jax import lax
from jax.experimental import pallas as pl
from jax.experimental.pallas import tpu as pltpu
from jax.sharding import PartitionSpec as P

MESH = pl.DeviceIdType.MESH
CHUNK = 128


def tile_of(extent):
    return next(t for t in (512, 384, 256, 128) if extent % t == 0)


def kernel(n_dp, n_rep, counts, grad, pre, up, down, ig_out, dg_out,
           gfull, hid, up_all, down_v, terms, from_core, from_x, from_z, masked, own_sum, other_sum,
           load_sem, gp_send, gp_recv, g_send, g_recv, p_send, p_recv, uy_send, u_send, u_recv, c_send, c_recv, x_send, x_recv, z_send, z_recv):
    rows, d_own = grad.shape
    ff = pre.shape[1]
    d_all = down.shape[0]
    n_z = n_dp // 4
    z_own = n_z // n_rep
    blk = d_all // n_dp
    n_chunks = rows // CHUNK
    ff_tile, d_tile = tile_of(ff), tile_of(d_all)
    slice_rows = n_dp
    while ff % (slice_rows * 16):
        slice_rows //= 2
    slice_cols = n_dp // slice_rows
    tall, wide = ff // slice_rows, d_all // slice_cols

    me = lax.axis_index("dp")
    rep = lax.axis_index("rep")
    my_z, my_x, my_c = me // 4, (me // 2) % 2, me % 2
    core_peer = {"dp": my_z * 4 + my_x * 2 + (1 - my_c)}
    x_peer = {"dp": my_z * 4 + (1 - my_x) * 2 + my_c}
    rep_peers = [lax.rem(rep + o, n_rep) for o in range(1, n_rep)]

    def z_peer(z):
        return {"dp": z * 4 + my_x * 2 + my_c}

    loads = [
        pltpu.make_async_copy(src, dst, load_sem.at[i])
        for i, (src, dst) in enumerate(
            ((grad, gfull.at[rep]), (pre, hid), (down, down_v), (up, up_all.at[rep])))
    ]
    for load in loads:
        load.start()

    barrier = pltpu.get_barrier_semaphore()
    peers = [{"rep": r} for r in rep_peers] + [core_peer, x_peer]
    peers += [z_peer(lax.rem(my_z + o, n_z)) for o in range(1, n_z)]
    for peer in peers:
        pl.semaphore_signal(barrier, inc=1, device_id=peer, device_id_type=MESH)
    pl.semaphore_wait(barrier, len(peers))

    def rows_of(c):
        return pl.ds(pl.multiple_of(c * CHUNK, CHUNK), CHUNK)

    last_cols = pl.ds((z_own - 1) * 4 * blk, 4 * blk)

    def grad_copy(c, o, source):
        return pltpu.make_async_remote_copy(
            src_ref=grad.at[rows_of(c), last_cols], dst_ref=gfull.at[source, rows_of(c), last_cols],
            send_sem=g_send.at[c, o], recv_sem=g_recv.at[c, source],
            device_id={"rep": lax.rem(rep + o, n_rep)}, device_id_type=MESH)

    def early_copy(part, o, source):
        cols = pl.ds(part * 4 * blk, 4 * blk)
        return pltpu.make_async_remote_copy(
            src_ref=grad.at[:, cols], dst_ref=gfull.at[source, :, cols],
            send_sem=gp_send.at[o, part], recv_sem=gp_recv.at[source, part],
            device_id={"rep": lax.rem(rep + o, n_rep)}, device_id_type=MESH)

    def part_copy(c, o, source):
        return pltpu.make_async_remote_copy(
            src_ref=masked.at[rep, rows_of(c)], dst_ref=masked.at[source, rows_of(c)],
            send_sem=p_send.at[c, o], recv_sem=p_recv.at[c, source],
            device_id={"rep": lax.rem(rep + o, n_rep)}, device_id_type=MESH)

    def slice_at(s):
        down_at = pl.ds(pl.multiple_of((s // slice_cols) * tall, tall), tall)
        if slice_cols == 1:
            return (down_at,)
        return (down_at, pl.ds(pl.multiple_of((s % slice_cols) * wide, wide), wide))

    def up_rep_copy(o, source):
        return pltpu.make_async_remote_copy(
            src_ref=up.at[slice_at(me)], dst_ref=up_all.at[(source,) + slice_at(me)],
            send_sem=uy_send.at[o], recv_sem=u_recv.at[source, me],
            device_id={"rep": lax.rem(rep + o, n_rep)}, device_id_type=MESH)

    def up_copy(g, s, stage, peer):
        block = up_all.at[(g,) + slice_at(s)]
        return pltpu.make_async_remote_copy(
            src_ref=block, dst_ref=block, send_sem=u_send.at[g, stage], recv_sem=u_recv.at[g, s],
            device_id=peer, device_id_type=MESH)

    def index_of(z, x, core):
        return z * 4 + x * 2 + core

    def along_z(g, z, stage, step):
        to = lax.rem(my_z + step + n_z, n_z)
        return up_copy(g, index_of(z, my_x, my_c), stage, z_peer(to))

    def over_x(g, z):
        return up_copy(g, index_of(z, my_x, my_c), n_z + z, x_peer)

    def over_core(g, z, x):
        return up_copy(g, index_of(z, x, my_c), 2 * n_z + 2 * z + x, core_peer)

    def landed(g, s):
        up_copy(g, s, 0, core_peer).wait_recv()

    for o in range(1, n_rep):
        up_rep_copy(o, rep).start()
    for part in range(z_own - 1):
        for o in range(1, n_rep):
            early_copy(part, o, rep).start()
    for c in range(n_chunks):
        for o in range(1, n_rep):
            grad_copy(c, o, rep).start()

    loads[1].wait()
    count = counts[0]

    def mask_rows(c, _):
        at = lax.broadcasted_iota(jnp.int32, (CHUNK, ff), 0) + c * CHUNK
        kept = jnp.where(at < count, hid[rows_of(c), :].astype(jnp.float32), 0.0)
        kept = jnp.maximum(kept, 0.0)
        hid[rows_of(c), :] = kept.astype(jnp.bfloat16)
        return 0

    lax.fori_loop(0, n_chunks, mask_rows, 0)
    loads[0].wait()

    def core_copy(z):
        return pltpu.make_async_remote_copy(
            src_ref=terms.at[z, 1 - my_c], dst_ref=from_core.at[z],
            send_sem=c_send.at[z], recv_sem=c_recv.at[z],
            device_id=core_peer, device_id_type=MESH)

    def x_copy(z):
        return pltpu.make_async_remote_copy(
            src_ref=from_core.at[z, 1 - my_x], dst_ref=from_x.at[z],
            send_sem=x_send.at[z], recv_sem=x_recv.at[z],
            device_id=x_peer, device_id_type=MESH)

    def z_copy(z, source):
        return pltpu.make_async_remote_copy(
            src_ref=from_x.at[z], dst_ref=from_z.at[source],
            send_sem=z_send.at[z], recv_sem=z_recv.at[source],
            device_id=z_peer(z), device_id_type=MESH)

    def z_at(k):
        late = k - z_own
        other = lax.rem(rep + 1 + lax.rem(late, n_rep - 1), n_rep) * z_own + late // (n_rep - 1)
        return jnp.where(k < z_own, rep * z_own + k, other)

    def make_terms(k, _):
        z = z_at(k)
        group = z // z_own
        cols = pl.ds(pl.multiple_of((z - group * z_own) * 4 * blk, 4 * blk), 4 * blk)

        def one(j, _):
            at = pl.ds(pl.multiple_of(j * ff_tile, ff_tile), ff_tile)
            out = lax.dot_general(
                gfull[group, :, cols], hid[:, at], (((0,), (0,)), ((), ())),
                preferred_element_type=jnp.float32).astype(jnp.bfloat16)
            for x in range(2):
                for core in range(2):
                    row = (x * 2 + core) * blk
                    terms[z, core, x, :, at] = out[row:row + blk]
            return 0

        lax.fori_loop(0, ff // ff_tile, one, 0)
        core_copy(z).start()
        return 0

    def add_core(k, _):
        z = z_at(k)
        core_copy(z).wait()
        for x in range(2):
            total = from_core[z, x].astype(jnp.float32) + terms[z, my_c, x].astype(jnp.float32)
            from_core[z, x] = total.astype(jnp.bfloat16)
        x_copy(z).start()
        return 0

    def add_x(k, _):
        z = z_at(k)
        x_copy(z).wait()
        total = from_x[z].astype(jnp.float32) + from_core[z, my_x].astype(jnp.float32)
        from_x[z] = total.astype(jnp.bfloat16)

        @pl.when(z != my_z)
        def _():
            z_copy(z, my_z).start()

        return 0

    def chunk(c, _):
        at_rows = rows_of(c)
        for o in range(1, n_rep):
            grad_copy(c, o, lax.rem(rep + o, n_rep)).wait_recv()

        def hidden_tile(j, _):
            at = pl.ds(pl.multiple_of(j * ff_tile, ff_tile), ff_tile)
            total = jnp.dot(gfull[0, at_rows, :], down_v[:d_own, at],
                            preferred_element_type=jnp.float32)
            for g in range(1, n_rep):
                total += jnp.dot(gfull[g, at_rows, :], down_v[g * d_own:(g + 1) * d_own, at],
                                 preferred_element_type=jnp.float32)
            passed = hid[at_rows, at].astype(jnp.float32) > 0.0
            masked[rep, at_rows, at] = jnp.where(passed, total, 0.0).astype(jnp.bfloat16)
            return 0

        lax.fori_loop(0, ff // ff_tile, hidden_tile, 0)

        for o in range(1, n_rep):
            part_copy(c, o, rep).start()
        if n_rep == 2:
            def own_tile(j, _):
                at = pl.ds(pl.multiple_of(j * d_tile, d_tile), d_tile)
                own_sum[at_rows, at] = jnp.dot(masked[rep, at_rows, :], up_all[rep, :, at],
                                               preferred_element_type=jnp.float32)
                return 0

            lax.fori_loop(0, d_all // d_tile, own_tile, 0)
        return 0

    def spread_start():
        for g in rep_peers:
            landed(g, me)
            over_x(g, my_z).start()
            over_core(g, my_z, my_x).start()

            @pl.when(my_z + 1 < n_z)
            def _():
                along_z(g, my_z, my_z, 1).start()

            @pl.when(my_z > 0)
            def _():
                along_z(g, my_z, n_dp, -1).start()

    def both_sides(d, visit):
        @pl.when(my_z >= d)
        def _():
            visit(my_z - d, my_z + 1 < n_z, 1)

        @pl.when(my_z + d < n_z)
        def _():
            visit(my_z + d, my_z > 0, -1)

    def spread_z(d, _):
        def visit(z, goes_on, step):
            for g in rep_peers:
                landed(g, index_of(z, my_x, my_c))

                @pl.when(goes_on)
                def _():
                    along_z(g, z, z, step).start()

                over_core(g, z, my_x).start()

        both_sides(d, visit)
        return 0

    def cross_x(d, _):
        def visit(z, goes_on, step):
            for g in rep_peers:
                over_x(g, z).start()

        both_sides(d, visit)
        return 0

    def pass_core(z):
        for g in rep_peers:
            landed(g, index_of(z, 1 - my_x, my_c))
            over_core(g, z, 1 - my_x).start()

    def spread_core(d, _):
        both_sides(d, lambda z, goes_on, step: pass_core(z))
        return 0

    def spread_end(z, _):
        for g in rep_peers:
            for x in range(2):
                landed(g, index_of(z, x, 1 - my_c))
        return 0

    def spread_sent(z, _):
        for g in rep_peers:
            over_x(g, z).wait_send()
            for x in range(2):
                over_core(g, z, x).wait_send()

            @pl.when((z <= my_z) & (my_z + 1 < n_z))
            def _():
                along_z(g, z, z, 1).wait_send()

            @pl.when((z > my_z) & (my_z > 0))
            def _():
                along_z(g, z, z, -1).wait_send()

            @pl.when((z == my_z) & (my_z > 0))
            def _():
                along_z(g, z, n_dp, -1).wait_send()

        return 0

    first_late, last_late = z_own, n_z - (n_rep - 1)
    third = max(n_chunks // 3, 1)
    lax.fori_loop(0, z_own, make_terms, 0)
    lax.fori_loop(0, z_own, add_core, 0)
    spread_start()
    for part in range(z_own - 1):
        for o in range(1, n_rep):
            early_copy(part, o, lax.rem(rep + o, n_rep)).wait_recv()
    lax.fori_loop(first_late, last_late, make_terms, 0)
    lax.fori_loop(first_late, last_late, add_core, 0)
    lax.fori_loop(1, 2, spread_z, 0)
    lax.fori_loop(1, 2, cross_x, 0)
    lax.fori_loop(0, z_own, add_x, 0)
    loads[2].wait()
    loads[3].wait()
    lax.fori_loop(0, third, chunk, 0)
    lax.fori_loop(first_late, last_late, add_x, 0)
    lax.fori_loop(third, 2 * third, chunk, 0)
    lax.fori_loop(2, 3, spread_z, 0)
    lax.fori_loop(2 * third, n_chunks, chunk, 0)
    lax.fori_loop(last_late, n_z, make_terms, 0)
    lax.fori_loop(last_late, n_z, add_core, 0)
    lax.fori_loop(2, 3, cross_x, 0)
    lax.fori_loop(last_late, n_z, add_x, 0)
    lax.fori_loop(3, n_z, spread_z, 0)
    lax.fori_loop(3, n_z, cross_x, 0)
    pass_core(my_z)
    lax.fori_loop(1, 2, spread_core, 0)
    lax.fori_loop(2, n_z, spread_core, 0)
    lax.fori_loop(0, n_z, spread_end, 0)

    def finish(c, _):
        at_rows = rows_of(c)
        for o in range(1, n_rep):
            part_copy(c, o, lax.rem(rep + o, n_rep)).wait_recv()

        def out_tile(j, _):
            at = pl.ds(pl.multiple_of(j * d_tile, d_tile), d_tile)

            def term(g):
                other_sum[...] = jnp.dot(masked[g, at_rows, :], up_all[g, :, at],
                                         preferred_element_type=jnp.float32)
                return other_sum[...]

            if n_rep == 2:
                total = own_sum[at_rows, at] + term(1 - rep)
            else:
                total = term(0)
                for g in range(1, n_rep):
                    total += term(g)
            ig_out[at_rows, at] = total.astype(jnp.bfloat16)
            return 0

        lax.fori_loop(0, d_all // d_tile, out_tile, 0)
        return 0

    lax.fori_loop(0, n_chunks - 1, finish, 0)

    total = from_x[my_z].astype(jnp.float32)
    for o in range(1, n_z):
        source = lax.rem(my_z + o, n_z)
        z_copy(source, source).wait()
        total += from_z[source].astype(jnp.float32)
    dg_out[...] = total / n_dp

    lax.fori_loop(n_chunks - 1, n_chunks, finish, 0)
    for c in range(n_chunks):
        for o in range(1, n_rep):
            grad_copy(c, o, rep).wait_send()
            part_copy(c, o, rep).wait_send()
    for part in range(z_own - 1):
        for o in range(1, n_rep):
            early_copy(part, o, rep).wait_send()
    for o in range(1, n_rep):
        up_rep_copy(o, rep).wait_send()
    lax.fori_loop(0, n_z, spread_sent, 0)


def on_device(n_dp, n_rep, grad_out, pre_act, up_weight, down_weight, slot_counts):
    rows, d_own = grad_out.shape
    ff = pre_act.shape[1]
    d_all = down_weight.shape[0]
    n_z = n_dp // 4
    blk = d_all // n_dp
    n_chunks = rows // CHUNK
    any_ref = pl.BlockSpec(memory_space=pl.ANY)
    bf16, dma = jnp.bfloat16, pltpu.SemaphoreType.DMA
    return pl.pallas_call(
        functools.partial(kernel, n_dp, n_rep),
        out_shape=(pltpu.VMEM((rows, d_all), bf16), pltpu.VMEM((blk, ff), jnp.float32)),
        in_specs=[pl.BlockSpec(memory_space=pltpu.SMEM)] + [any_ref] * 4,
        out_specs=(pl.BlockSpec(memory_space=pltpu.VMEM),) * 2,
        scratch_shapes=[
            pltpu.VMEM((n_rep, rows, d_own), bf16),
            pltpu.VMEM((rows, ff), bf16),
            pltpu.VMEM((n_rep, ff, d_all), bf16),
            pltpu.VMEM((d_all, ff), bf16),
            pltpu.VMEM((n_z, 2, 2, blk, ff), bf16),
            pltpu.VMEM((n_z, 2, blk, ff), bf16),
            pltpu.VMEM((n_z, blk, ff), bf16),
            pltpu.VMEM((n_z, blk, ff), bf16),
            pltpu.VMEM((n_rep, rows, ff), bf16),
            pltpu.VMEM((rows, d_all), jnp.float32),
            pltpu.VMEM((CHUNK, tile_of(d_all)), jnp.float32),
            dma((4,)), dma((n_rep, n_z)), dma((n_rep, n_z)),
            dma((n_chunks, n_rep)), dma((n_chunks, n_rep)),
            dma((n_chunks, n_rep)), dma((n_chunks, n_rep)),
            dma((n_rep,)), dma((n_rep, n_dp + 1)), dma((n_rep, n_dp)),
            dma((n_z,)), dma((n_z,)), dma((n_z,)), dma((n_z,)), dma((n_z,)), dma((n_z,)),
        ],
        compiler_params=pltpu.CompilerParams(
            collective_id=0, has_side_effects=True, vmem_limit_bytes=54 * 2**20),
    )(slot_counts, grad_out, pre_act, up_weight, down_weight)


def solution(mesh):
    sizes = dict(mesh.shape)
    return jax.shard_map(
        functools.partial(on_device, sizes["dp"], sizes["rep"]),
        mesh=mesh,
        in_specs=(P("dp", "rep"), P("dp", "rep"), P("rep", None), P(None, "rep"), P("dp")),
        out_specs=(P("dp", None), P("dp", "rep")),
        check_vma=False,
    )
```

profile of v0, /device:TPU:0, one launch (start us, length us, event | category | flops | bytes accessed | tf_op | source)
XLA Modules:
  0.0 110.3 jit_solution(14805717645202710123)
XLA Ops:
  1.3 106.4 %shard_map.68 = (bf16[768,2048]{1,0:T(8,128)(2,1)S(1)}, f32[128,1536]{1,0:T(8,128)S(1)}) custom-call(s32[1]{0:T(128)S(6)} %copy.11.counts, bf16[768,1024]{1,0:T(8,128)(2,1)} %grad.1, bf16[768,1536]{1,0:T(8,128)(2,1)} %pre.1, bf16[1536,2048]{1,0:T(8,128)(2,1)} %up.1, bf16[2048,1536]{1,0:T(8,128)(2,1)} %down.1), custom_call_target="tpu_custom_call" | custom-call | tf_op jit(solution)/shard_map/pallas_call | solution.py:401
  107.7 1.7 %copy.9 = bf16[768,2048]{1,0:T(8,128)(2,1)} copy(bf16[768,2048]{1,0:T(8,128)(2,1)S(1)} %get-tuple-element.2) | data formatting | bytes 6291456
  109.4 0.9 copy.10
where the time goes:
time: 111 us; the launch traced here: 110 us
  Pallas kernels  106 us (95%)
  local copies, waits for them, and re-layouts  2.55 us (2%)
  between operations  1.29 us (1%)
    pallas_call x1, Pallas kernels, on_device(): pl.pallas_call(functools.partial(kernel, n_dp, n_rep), out_shape=(pltpu.V...  106 us
    unnamed x2, local copies, waits for them, and re-layouts  2.55 us

commit v1 on v0

v1 whole, which is shorter than its diff:
```python
import functools

import jax
import jax.numpy as jnp
from jax import lax
from jax.experimental import pallas as pl
from jax.experimental.pallas import tpu as pltpu
from jax.sharding import PartitionSpec as P

MESH = pl.DeviceIdType.MESH
CHUNK = 128


def tile_of(extent):
    return next(t for t in (512, 384, 256, 128) if extent % t == 0)


def kernel(n_dp, n_rep, counts, grad, pre, up, down, ig_out, dg_out,
           gfull, hid, up_all, down_v, terms, from_core, from_x, from_z, masked, own_sum, other_sum,
           far_sem, load_sem, gp_send, gp_recv, g_send, g_recv, p_send, p_recv, uy_send, u_send, u_recv,
           c_send, c_recv, x_send, x_recv, z_send, z_recv):
    rows, d_own = grad.shape
    ff = pre.shape[1]
    d_all = down.shape[0]
    n_z = n_dp // 4
    z_own = n_z // n_rep
    blk = d_all // n_dp
    n_chunks = rows // CHUNK
    ff_tile, d_tile = tile_of(ff), tile_of(d_all)
    n_tiles = ff // ff_tile
    slice_rows = n_dp
    while ff % (slice_rows * 16):
        slice_rows //= 2
    slice_cols = n_dp // slice_rows
    tall, wide = ff // slice_rows, d_all // slice_cols

    me = lax.axis_index("dp")
    rep = lax.axis_index("rep")
    my_z, my_x, my_c = me // 4, (me // 2) % 2, me % 2
    core_peer = {"dp": my_z * 4 + my_x * 2 + (1 - my_c)}
    x_peer = {"dp": my_z * 4 + (1 - my_x) * 2 + my_c}
    rep_peers = [lax.rem(rep + o, n_rep) for o in range(1, n_rep)]
    above, below = my_z + 1 < n_z, my_z > 0

    def z_peer(z):
        return {"dp": z * 4 + my_x * 2 + my_c}

    def signal(sem, peer):
        pl.semaphore_signal(sem, inc=1, device_id=peer, device_id_type=MESH)

    barrier = pltpu.get_barrier_semaphore()
    near = [{"rep": r} for r in rep_peers] + [core_peer, x_peer]
    for peer in near:
        signal(barrier, peer)
    pl.when(above)(lambda: signal(barrier, z_peer(my_z + 1)))
    pl.when(below)(lambda: signal(barrier, z_peer(my_z - 1)))

    loads = [
        pltpu.make_async_copy(src, dst, load_sem.at[i])
        for i, (src, dst) in enumerate(
            ((grad, gfull.at[rep]), (pre, hid), (down, down_v), (up, up_all.at[rep])))
    ]
    loads[1].start()
    loads[0].start()
    pl.semaphore_wait(barrier, len(near) + above.astype(jnp.int32) + below.astype(jnp.int32))

    def rows_of(c):
        return pl.ds(pl.multiple_of(c * CHUNK, CHUNK), CHUNK)

    last_cols = pl.ds((z_own - 1) * 4 * blk, 4 * blk)

    def grad_copy(c, o, source):
        return pltpu.make_async_remote_copy(
            src_ref=grad.at[rows_of(c), last_cols], dst_ref=gfull.at[source, rows_of(c), last_cols],
            send_sem=g_send.at[c, o], recv_sem=g_recv.at[c, source],
            device_id={"rep": lax.rem(rep + o, n_rep)}, device_id_type=MESH)

    def early_copy(part, o, source):
        cols = pl.ds(part * 4 * blk, 4 * blk)
        return pltpu.make_async_remote_copy(
            src_ref=grad.at[:, cols], dst_ref=gfull.at[source, :, cols],
            send_sem=gp_send.at[o, part], recv_sem=gp_recv.at[source, part],
            device_id={"rep": lax.rem(rep + o, n_rep)}, device_id_type=MESH)

    def tile_at(j):
        return pl.ds(pl.multiple_of(j * ff_tile, ff_tile), ff_tile)

    def part_copy(c, j, o, source):
        return pltpu.make_async_remote_copy(
            src_ref=masked.at[rep, rows_of(c), tile_at(j)], dst_ref=masked.at[source, rows_of(c), tile_at(j)],
            send_sem=p_send.at[c * n_tiles + j, o], recv_sem=p_recv.at[c * n_tiles + j, source],
            device_id={"rep": lax.rem(rep + o, n_rep)}, device_id_type=MESH)

    def slice_at(s):
        down_at = pl.ds(pl.multiple_of((s // slice_cols) * tall, tall), tall)
        if slice_cols == 1:
            return (down_at,)
        return (down_at, pl.ds(pl.multiple_of((s % slice_cols) * wide, wide), wide))

    def up_rep_copy(o, source):
        return pltpu.make_async_remote_copy(
            src_ref=up.at[slice_at(me)], dst_ref=up_all.at[(source,) + slice_at(me)],
            send_sem=uy_send.at[o], recv_sem=u_recv.at[source, me],
            device_id={"rep": lax.rem(rep + o, n_rep)}, device_id_type=MESH)

    def up_copy(g, s, stage, peer):
        block = up_all.at[(g,) + slice_at(s)]
        return pltpu.make_async_remote_copy(
            src_ref=block, dst_ref=block, send_sem=u_send.at[g, stage], recv_sem=u_recv.at[g, s],
            device_id=peer, device_id_type=MESH)

    def index_of(z, x, core):
        return z * 4 + x * 2 + core

    def along_z(g, z, x, step):
        to = lax.rem(my_z + step + n_z, n_z)
        stage = z * 2 + x
        if step < 0:
            stage = jnp.where(z == my_z, 2 * n_z + x, stage)
        return up_copy(g, index_of(z, x, my_c), stage, z_peer(to))

    def over_x(g):
        return up_copy(g, me, 2 * n_z + 2, x_peer)

    def over_core(g, z, x):
        return up_copy(g, index_of(z, x, my_c), 2 * n_z + 3 + 2 * z + x, core_peer)

    def landed(g, s):
        up_copy(g, s, 0, core_peer).wait_recv()

    for o in range(1, n_rep):
        up_rep_copy(o, rep).start()
    for part in range(z_own - 1):
        for o in range(1, n_rep):
            early_copy(part, o, rep).start()
    for c in range(n_chunks):
        for o in range(1, n_rep):
            grad_copy(c, o, rep).start()
    loads[2].start()
    loads[3].start()
    pl.when(my_z == 0)(lambda: signal(far_sem.at[0], z_peer(my_z + 1)))
    pl.when(my_z == n_z - 1)(lambda: signal(far_sem.at[1], z_peer(my_z - 1)))

    loads[1].wait()
    count = counts[0]

    def mask_rows(c, _):
        at = lax.broadcasted_iota(jnp.int32, (CHUNK, ff), 0) + c * CHUNK
        kept = jnp.where(at < count, hid[rows_of(c), :].astype(jnp.float32), 0.0)
        kept = jnp.maximum(kept, 0.0)
        hid[rows_of(c), :] = kept.astype(jnp.bfloat16)
        return 0

    lax.fori_loop(0, n_chunks, mask_rows, 0)
    loads[0].wait()

    def know_line():
        @pl.when(below)
        def _():
            pl.semaphore_wait(far_sem.at[0], 1)
            pl.when(above)(lambda: signal(far_sem.at[0], z_peer(my_z + 1)))

        @pl.when(above)
        def _():
            pl.semaphore_wait(far_sem.at[1], 1)
            pl.when(below)(lambda: signal(far_sem.at[1], z_peer(my_z - 1)))

    def core_copy(z):
        return pltpu.make_async_remote_copy(
            src_ref=terms.at[z, 1 - my_c], dst_ref=from_core.at[z],
            send_sem=c_send.at[z], recv_sem=c_recv.at[z],
            device_id=core_peer, device_id_type=MESH)

    def x_copy(z):
        return pltpu.make_async_remote_copy(
            src_ref=from_core.at[z, 1 - my_x], dst_ref=from_x.at[z],
            send_sem=x_send.at[z], recv_sem=x_recv.at[z],
            device_id=x_peer, device_id_type=MESH)

    def z_copy(z, source):
        return pltpu.make_async_remote_copy(
            src_ref=from_x.at[z], dst_ref=from_z.at[source],
            send_sem=z_send.at[z], recv_sem=z_recv.at[source],
            device_id=z_peer(z), device_id_type=MESH)

    def z_at(k):
        late = k - z_own
        other = lax.rem(rep + 1 + lax.rem(late, n_rep - 1), n_rep) * z_own + late // (n_rep - 1)
        return jnp.where(k < z_own, rep * z_own + k, other)

    def make_terms(k, _):
        z = z_at(k)
        group = z // z_own
        cols = pl.ds(pl.multiple_of((z - group * z_own) * 4 * blk, 4 * blk), 4 * blk)

        def one(j, _):
            at = tile_at(j)
            out = lax.dot_general(
                gfull[group, :, cols], hid[:, at], (((0,), (0,)), ((), ())),
                preferred_element_type=jnp.float32).astype(jnp.bfloat16)
            for x in range(2):
                for core in range(2):
                    row = (x * 2 + core) * blk
                    terms[z, core, x, :, at] = out[row:row + blk]
            return 0

        lax.fori_loop(0, n_tiles, one, 0)
        core_copy(z).start()
        return 0

    def add_core(k, _):
        z = z_at(k)
        core_copy(z).wait()
        for x in range(2):
            total = from_core[z, x].astype(jnp.float32) + terms[z, my_c, x].astype(jnp.float32)
            from_core[z, x] = total.astype(jnp.bfloat16)
        x_copy(z).start()
        return 0

    def add_x(k, _):
        z = z_at(k)
        x_copy(z).wait()
        total = from_x[z].astype(jnp.float32) + from_core[z, my_x].astype(jnp.float32)
        from_x[z] = total.astype(jnp.bfloat16)

        @pl.when(z != my_z)
        def _():
            z_copy(z, my_z).start()

        return 0

    def chunk(c, _):
        at_rows = rows_of(c)
        for o in range(1, n_rep):
            grad_copy(c, o, lax.rem(rep + o, n_rep)).wait_recv()

        def hidden_tile(j, _):
            at = tile_at(j)
            total = jnp.dot(gfull[0, at_rows, :], down_v[:d_own, at],
                            preferred_element_type=jnp.float32)
            for g in range(1, n_rep):
                total += jnp.dot(gfull[g, at_rows, :], down_v[g * d_own:(g + 1) * d_own, at],
                                 preferred_element_type=jnp.float32)
            passed = hid[at_rows, at].astype(jnp.float32) > 0.0
            masked[rep, at_rows, at] = jnp.where(passed, total, 0.0).astype(jnp.bfloat16)
            for o in range(1, n_rep):
                part_copy(c, j, o, rep).start()
            return 0

        lax.fori_loop(0, n_tiles, hidden_tile, 0)
        return 0

    def start_line(g, x):
        pl.when(above)(lambda: along_z(g, my_z, x, 1).start())
        pl.when(below)(lambda: along_z(g, my_z, x, -1).start())

    def spread_start():
        for g in rep_peers:
            landed(g, me)
            over_x(g).start()
            start_line(g, my_x)
            over_core(g, my_z, my_x).start()

    def spread_x():
        for g in rep_peers:
            landed(g, index_of(my_z, 1 - my_x, my_c))
            start_line(g, 1 - my_x)
            over_core(g, my_z, 1 - my_x).start()

    def spread_z(d, x):
        def visit(z, goes_on, step):
            for g in rep_peers:
                landed(g, index_of(z, x, my_c))
                pl.when(goes_on)(lambda: along_z(g, z, x, step).start())
                over_core(g, z, x).start()

        pl.when(my_z >= d)(lambda: visit(my_z - d, above, 1))
        pl.when(my_z + d < n_z)(lambda: visit(my_z + d, below, -1))

    def spread_rest(d, _):
        spread_z(d, my_x)
        spread_z(d, 1 - my_x)
        return 0

    def spread_end(z, _):
        for g in rep_peers:
            for x in range(2):
                landed(g, index_of(z, x, 1 - my_c))
        return 0

    def spread_sent(z, _):
        for g in rep_peers:
            for x in range(2):
                over_core(g, z, x).wait_send()
                pl.when((z <= my_z) & above)(lambda: along_z(g, z, x, 1).wait_send())
                pl.when((z >= my_z) & below)(lambda: along_z(g, z, x, -1).wait_send())
        return 0

    def finish(c, _):
        at_rows = rows_of(c)

        def arrived(j, _):
            for o in range(1, n_rep):
                part_copy(c, j, o, lax.rem(rep + o, n_rep)).wait_recv()
            return 0

        lax.fori_loop(0, n_tiles, arrived, 0)

        def out_tile(j, _):
            at = pl.ds(pl.multiple_of(j * d_tile, d_tile), d_tile)
            total = jnp.dot(masked[0, at_rows, :], up_all[0, :, at], preferred_element_type=jnp.float32)
            for g in range(1, n_rep):
                total += jnp.dot(masked[g, at_rows, :], up_all[g, :, at], preferred_element_type=jnp.float32)
            ig_out[at_rows, at] = total.astype(jnp.bfloat16)
            return 0

        lax.fori_loop(0, d_all // d_tile, out_tile, 0)
        return 0

    tail = n_chunks - 1
    tail_rows = rows_of(tail)

    def tail_term(g, j, into):
        def one(i, _):
            at = pl.ds(pl.multiple_of(i * d_tile, d_tile), d_tile)
            part = jnp.dot(masked[g, tail_rows, tile_at(j)], up_all[g, tile_at(j), at],
                           preferred_element_type=jnp.float32)

            @pl.when(j == 0)
            def _():
                into[:, at] = part

            @pl.when(j > 0)
            def _():
                into[:, at] += part

            return 0

        lax.fori_loop(0, d_all // d_tile, one, 0)

    def own_tail(j, _):
        tail_term(rep, j, own_sum)
        return 0

    def other_tail(j, _):
        part_copy(tail, j, 1, 1 - rep).wait_recv()
        tail_term(1 - rep, j, other_sum)
        return 0

    first_late, last_late = z_own, n_z - (n_rep - 1)
    third = max(n_chunks // 3, 1)
    lax.fori_loop(0, z_own, make_terms, 0)
    lax.fori_loop(0, 1, add_core, 0)
    spread_start()
    lax.fori_loop(1, z_own, add_core, 0)
    know_line()
    lax.fori_loop(0, 1, add_x, 0)
    spread_z(1, my_x)
    for part in range(z_own - 1):
        for o in range(1, n_rep):
            early_copy(part, o, lax.rem(rep + o, n_rep)).wait_recv()
    lax.fori_loop(first_late, last_late, make_terms, 0)
    spread_x()
    lax.fori_loop(first_late, last_late, add_core, 0)
    loads[2].wait()
    lax.fori_loop(0, third, chunk, 0)
    if n_z > 2:
        spread_z(2, my_x)
    lax.fori_loop(1, z_own, add_x, 0)
    lax.fori_loop(third, 2 * third, chunk, 0)
    spread_z(1, 1 - my_x)
    lax.fori_loop(2 * third, n_chunks, chunk, 0)
    lax.fori_loop(last_late, n_z, make_terms, 0)
    lax.fori_loop(first_late, last_late, add_x, 0)
    lax.fori_loop(last_late, n_z, add_core, 0)
    if n_z > 3:
        spread_z(3, my_x)
    if n_z > 2:
        spread_z(2, 1 - my_x)
    if n_z > 3:
        spread_z(3, 1 - my_x)
    lax.fori_loop(4, n_z, spread_rest, 0)
    loads[3].wait()
    if n_rep == 2:
        lax.fori_loop(0, n_tiles, own_tail, 0)
    lax.fori_loop(last_late, n_z, add_x, 0)
    lax.fori_loop(0, n_z, spread_end, 0)
    lax.fori_loop(0, tail, finish, 0)

    total = from_x[my_z].astype(jnp.float32)
    for o in range(1, n_z):
        source = lax.rem(my_z + o, n_z)
        z_copy(source, source).wait()
        total += from_z[source].astype(jnp.float32)
    dg_out[...] = total / n_dp

    for o in range(1, n_rep):
        for part in range(z_own - 1):
            early_copy(part, o, rep).wait_send()
        up_rep_copy(o, rep).wait_send()
    for g in rep_peers:
        over_x(g).wait_send()
    lax.fori_loop(0, n_z, spread_sent, 0)

    if n_rep == 2:
        lax.fori_loop(0, n_tiles, other_tail, 0)
        ig_out[tail_rows, :] = (own_sum[...] + other_sum[...]).astype(jnp.bfloat16)
    else:
        lax.fori_loop(tail, n_chunks, finish, 0)

    def sent(c, _):
        for o in range(1, n_rep):
            grad_copy(c, o, rep).wait_send()
            for j in range(n_tiles):
                part_copy(c, j, o, rep).wait_send()
        return 0

    lax.fori_loop(0, n_chunks, sent, 0)


def store(n_parts, ig, dg, ig_out, dg_out, sem):
    part = ig.shape[0] // n_parts
    copies = [pltpu.make_async_copy(ig.at[pl.ds(i * part, part)], ig_out.at[pl.ds(i * part, part)], sem.at[i])
              for i in range(n_parts)]
    copies.append(pltpu.make_async_copy(dg, dg_out, sem.at[n_parts]))
    for copy in copies:
        copy.start()
    for copy in copies:
        copy.wait()


def on_device(n_dp, n_rep, grad_out, pre_act, up_weight, down_weight, slot_counts):
    rows, d_own = grad_out.shape
    ff = pre_act.shape[1]
    d_all = down_weight.shape[0]
    n_z = n_dp // 4
    blk = d_all // n_dp
    n_chunks = rows // CHUNK
    n_pieces = n_chunks * (ff // tile_of(ff))
    any_ref = pl.BlockSpec(memory_space=pl.ANY)
    in_vmem = pl.BlockSpec(memory_space=pltpu.VMEM)
    bf16, dma = jnp.bfloat16, pltpu.SemaphoreType.DMA
    results = pl.pallas_call(
        functools.partial(kernel, n_dp, n_rep),
        out_shape=(pltpu.VMEM((rows, d_all), bf16), pltpu.VMEM((blk, ff), jnp.float32)),
        in_specs=[pl.BlockSpec(memory_space=pltpu.SMEM)] + [any_ref] * 4,
        out_specs=(in_vmem,) * 2,
        scratch_shapes=[
            pltpu.VMEM((n_rep, rows, d_own), bf16),
            pltpu.VMEM((rows, ff), bf16),
            pltpu.VMEM((n_rep, ff, d_all), bf16),
            pltpu.VMEM((d_all, ff), bf16),
            pltpu.VMEM((n_z, 2, 2, blk, ff), bf16),
            pltpu.VMEM((n_z, 2, blk, ff), bf16),
            pltpu.VMEM((n_z, blk, ff), bf16),
            pltpu.VMEM((n_z, blk, ff), bf16),
            pltpu.VMEM((n_rep, rows, ff), bf16),
            pltpu.VMEM((CHUNK, d_all), jnp.float32),
            pltpu.VMEM((CHUNK, d_all), jnp.float32),
            pltpu.SemaphoreType.REGULAR((2,)),
            dma((4,)), dma((n_rep, n_z)), dma((n_rep, n_z)),
            dma((n_chunks, n_rep)), dma((n_chunks, n_rep)),
            dma((n_pieces, n_rep)), dma((n_pieces, n_rep)),
            dma((n_rep,)), dma((n_rep, n_dp + 3)), dma((n_rep, n_dp)),
            dma((n_z,)), dma((n_z,)), dma((n_z,)), dma((n_z,)), dma((n_z,)), dma((n_z,)),
        ],
        compiler_params=pltpu.CompilerParams(
            collective_id=0, has_side_effects=True, vmem_limit_bytes=54 * 2**20),
    )(slot_counts, grad_out, pre_act, up_weight, down_weight)
    n_parts = 4
    return pl.pallas_call(
        functools.partial(store, n_parts),
        out_shape=(jax.ShapeDtypeStruct((rows, d_all), bf16), jax.ShapeDtypeStruct((blk, ff), jnp.float32)),
        in_specs=[in_vmem] * 2,
        out_specs=(any_ref,) * 2,
        scratch_shapes=[dma((n_parts + 1,))],
        compiler_params=pltpu.CompilerParams(vmem_limit_bytes=6 * 2**20),
    )(*results)


def solution(mesh):
    sizes = dict(mesh.shape)
    return jax.shard_map(
        functools.partial(on_device, sizes["dp"], sizes["rep"]),
        mesh=mesh,
        in_specs=(P("dp", "rep"), P("dp", "rep"), P("rep", None), P(None, "rep"), P("dp")),
        out_specs=(P("dp", None), P("dp", "rep")),
        check_vma=False,
    )
```

time: 111 us -> 120 us (1.081)
  the two profiles are of different devices: /device:TPU:0 before, /device:TPU:28 now
where the time goes in v1:
time: 120 us
  Pallas kernels  118 us (98%)
  between operations  1.29 us (1%)
    pallas_call x1, Pallas kernels, on_device(): pl.pallas_call(functools.partial(kernel, n_dp, n_rep), out_shape=(pltpu.V...  116 us

profile of v1, /device:TPU:28, one launch (start us, length us, event | category | flops | bytes accessed | tf_op | source)
XLA Modules:
  0.0 119.7 jit_solution(3423077748762653501)
XLA Ops:
  1.3 116.4 %shard_map.68 = (bf16[768,2048]{1,0:T(8,128)(2,1)S(1)}, f32[128,1536]{1,0:T(8,128)S(1)}) custom-call(s32[1]{0:T(128)S(6)} %copy.7.counts, bf16[768,1024]{1,0:T(8,128)(2,1)} %grad.1, bf16[768,1536]{1,0:T(8,128)(2,1)} %pre.1, bf16[1536,2048]{1,0:T(8,128)(2,1)} %up.1, bf16[2048,1536]{1,0:T(8,128)(2,1)} %down.1), custom_call_target="tpu_custom_call" | custom-call | tf_op jit(solution)/shard_map/pallas_call | solution.py:443
  117.7 2.0 %shard_map.69 = (bf16[768,2048]{1,0:T(8,128)(2,1)}, f32[128,1536]{1,0:T(8,128)}) custom-call(bf16[768,2048]{1,0:T(8,128)(2,1)S(1)} %get-tuple-element.4.ig, f32[128,1536]{1,0:T(8,128)S(1)} %get-tuple-element.5.dg), custom_call_target="tpu_custom_call" | custom-call | tf_op jit(solution)/shard_map/pallas_call | solution.py:471

commit v2 on v1

v2 whole, which is shorter than its diff:
```python
import functools

import jax
import jax.numpy as jnp
from jax import lax
from jax.experimental import pallas as pl
from jax.experimental.pallas import tpu as pltpu
from jax.sharding import PartitionSpec as P

MESH = pl.DeviceIdType.MESH
CHUNK = 128


def tile_of(extent):
    return next(t for t in (512, 384, 256, 128) if extent % t == 0)


def piece_of(extent):
    return next(t for t in (256, 128) if extent % t == 0)


def kernel(n_dp, n_rep, counts, grad, pre, up, down, ig_out, dg_out,
           gfull, hid, up_all, down_v, terms, from_core, from_x, from_z, masked, own_sum, other_sum,
           far_sem, load_sem, gp_send, gp_recv, g_send, g_recv, p_send, p_recv, t_recv, uy_send, uz_send, ux_send,
           uc_send, u_recv, uc_recv, c_send, c_recv, x_send, x_recv, z_send, z_recv):
    rows, d_own = grad.shape
    ff = pre.shape[1]
    d_all = down.shape[0]
    n_z = n_dp // 4
    z_own = n_z // n_rep
    blk = d_all // n_dp
    n_chunks = rows // CHUNK
    ff_tile, d_tile = tile_of(ff), tile_of(d_all)
    n_tiles = ff // ff_tile
    piece = piece_of(ff)
    n_pieces = ff // piece
    slice_rows = n_dp
    while ff % (slice_rows * 16):
        slice_rows //= 2
    slice_cols = n_dp // slice_rows
    tall, wide = ff // slice_rows, d_all // slice_cols

    me = lax.axis_index("dp")
    rep = lax.axis_index("rep")
    my_z, my_x, my_c = me // 4, (me // 2) % 2, me % 2
    core_peer = {"dp": my_z * 4 + my_x * 2 + (1 - my_c)}
    x_peer = {"dp": my_z * 4 + (1 - my_x) * 2 + my_c}
    offsets = range(1, n_rep)
    above, below = my_z + 1 < n_z, my_z > 0

    def ahead(o):
        return lax.rem(rep + o, n_rep)

    def behind(o):
        return lax.rem(rep + n_rep - o, n_rep)

    def send(src, dst, send_sem, recv_sem, peer):
        return pltpu.make_async_remote_copy(src_ref=src, dst_ref=dst, send_sem=send_sem, recv_sem=recv_sem,
                                            device_id=peer, device_id_type=MESH)

    def all_of(ref, sem):
        pltpu.make_async_copy(ref, ref, sem).wait()

    def z_peer(z):
        return {"dp": z * 4 + my_x * 2 + my_c}

    def signal(sem, peer):
        pl.semaphore_signal(sem, inc=1, device_id=peer, device_id_type=MESH)

    barrier = pltpu.get_barrier_semaphore()
    near = [{"rep": ahead(o)} for o in offsets] + [core_peer, x_peer]
    for peer in near:
        signal(barrier, peer)
    pl.when(above)(lambda: signal(barrier, z_peer(my_z + 1)))
    pl.when(below)(lambda: signal(barrier, z_peer(my_z - 1)))

    loads = [
        pltpu.make_async_copy(src, dst, load_sem.at[i])
        for i, (src, dst) in enumerate(
            ((grad, gfull.at[rep]), (pre, hid), (down, down_v), (up, up_all.at[rep])))
    ]
    loads[1].start()
    loads[0].start()
    pl.semaphore_wait(barrier, len(near) + above.astype(jnp.int32) + below.astype(jnp.int32))

    def rows_of(c):
        return pl.ds(pl.multiple_of(c * CHUNK, CHUNK), CHUNK)

    last_cols = pl.ds((z_own - 1) * 4 * blk, 4 * blk)

    def grad_copy(c, o, source):
        return send(grad.at[rows_of(c), last_cols], gfull.at[source, rows_of(c), last_cols],
                    g_send.at[o - 1], g_recv.at[c, o - 1], {"rep": ahead(o)})

    def early_copy(part, o, source):
        cols = pl.ds(part * 4 * blk, 4 * blk)
        return send(grad.at[:, cols], gfull.at[source, :, cols],
                    gp_send.at[part, o - 1], gp_recv.at[part, o - 1], {"rep": ahead(o)})

    def tile_at(j):
        return pl.ds(pl.multiple_of(j * ff_tile, ff_tile), ff_tile)

    def piece_at(j):
        return pl.ds(pl.multiple_of(j * piece, piece), piece)

    def part_copy(c, j, o):
        block = masked.at[rep, rows_of(c), tile_at(j)]
        return send(block, block, p_send.at[o - 1], p_recv.at[c, o - 1], {"rep": ahead(o)})

    def tail_copy(j, o):
        block = masked.at[rep, tail_rows, piece_at(j)]
        return send(block, block, p_send.at[o - 1], t_recv.at[j, o - 1], {"rep": ahead(o)})

    def tail_arrived(j, o):
        all_of(masked.at[behind(o), tail_rows, piece_at(j)], t_recv.at[j, o - 1])

    def slice_at(s):
        down_at = pl.ds(pl.multiple_of((s // slice_cols) * tall, tall), tall)
        if slice_cols == 1:
            return (down_at,)
        return (down_at, pl.ds(pl.multiple_of((s % slice_cols) * wide, wide), wide))

    def index_of(z, x, core):
        return z * 4 + x * 2 + core

    def up_rep_copy(o):
        return send(up.at[slice_at(me)], up_all.at[(rep,) + slice_at(me)],
                    uy_send.at[o - 1], u_recv.at[my_z * 2 + my_x, o - 1], {"rep": ahead(o)})

    def up_copy(o, s, send_sem, peer):
        block = up_all.at[(behind(o),) + slice_at(s)]
        return send(block, block, send_sem, u_recv.at[s // 2, o - 1], peer)

    def along_z(o, z, step):
        to = lax.rem(my_z + step + n_z, n_z)
        stage = z if step > 0 else jnp.where(z == my_z, n_z, z)
        return up_copy(o, index_of(z, my_x, my_c), uz_send.at[stage, o - 1], z_peer(to))

    def over_x(o, z):
        return up_copy(o, index_of(z, my_x, my_c), ux_send.at[o - 1], x_peer)

    def over_core(o, z, x):
        block = up_all.at[(behind(o),) + slice_at(index_of(z, x, my_c))]
        return send(block, block, uc_send.at[o - 1], uc_recv.at[o - 1], core_peer)

    def landed(o, z, x):
        up_copy(o, index_of(z, x, my_c), ux_send.at[o - 1], x_peer).wait_recv()

    for o in offsets:
        up_rep_copy(o).start()
    for part in range(z_own - 1):
        for o in offsets:
            early_copy(part, o, rep).start()
    for c in range(n_chunks):
        for o in offsets:
            grad_copy(c, o, rep).start()
    pl.when(my_z == 0)(lambda: signal(far_sem.at[0], z_peer(my_z + 1)))
    pl.when(my_z == n_z - 1)(lambda: signal(far_sem.at[1], z_peer(my_z - 1)))

    loads[1].wait()
    count = counts[0]

    def mask_rows(c, _):
        at = lax.broadcasted_iota(jnp.int32, (CHUNK, ff), 0) + c * CHUNK
        kept = jnp.where(at < count, hid[rows_of(c), :].astype(jnp.float32), 0.0)
        kept = jnp.maximum(kept, 0.0)
        hid[rows_of(c), :] = kept.astype(jnp.bfloat16)
        return 0

    lax.fori_loop(0, n_chunks, mask_rows, 0)
    loads[0].wait()

    def know_line():
        @pl.when(below)
        def _():
            pl.semaphore_wait(far_sem.at[0], 1)
            pl.when(above)(lambda: signal(far_sem.at[0], z_peer(my_z + 1)))

        @pl.when(above)
        def _():
            pl.semaphore_wait(far_sem.at[1], 1)
            pl.when(below)(lambda: signal(far_sem.at[1], z_peer(my_z - 1)))

    def core_copy(z):
        return send(terms.at[z, 1 - my_c], from_core.at[z], c_send, c_recv.at[z], core_peer)

    def x_copy(z):
        return send(from_core.at[z, 1 - my_x], from_x.at[z], x_send, x_recv.at[z], x_peer)

    def z_copy(z, source):
        slot = jnp.where(source > z, source - 1, source)
        return send(from_x.at[z], from_z.at[slot], z_send, z_recv, z_peer(z))

    def z_at(k):
        late = k - z_own
        other = lax.rem(rep + 1 + lax.rem(late, n_rep - 1), n_rep) * z_own + late // (n_rep - 1)
        return jnp.where(k < z_own, rep * z_own + k, other)

    def make_terms(k, _):
        z = z_at(k)
        group = z // z_own
        cols = pl.ds(pl.multiple_of((z - group * z_own) * 4 * blk, 4 * blk), 4 * blk)

        def one(j, _):
            at = tile_at(j)
            out = lax.dot_general(
                gfull[group, :, cols], hid[:, at], (((0,), (0,)), ((), ())),
                preferred_element_type=jnp.float32).astype(jnp.bfloat16)
            for x in range(2):
                for core in range(2):
                    row = (x * 2 + core) * blk
                    terms[z, core, x, :, at] = out[row:row + blk]
            return 0

        lax.fori_loop(0, n_tiles, one, 0)
        core_copy(z).start()
        return 0

    def add_core(k, _):
        z = z_at(k)
        core_copy(z).wait_recv()
        for x in range(2):
            total = from_core[z, x].astype(jnp.float32) + terms[z, my_c, x].astype(jnp.float32)
            from_core[z, x] = total.astype(jnp.bfloat16)
        x_copy(z).start()
        return 0

    def add_x(k, _):
        z = z_at(k)
        x_copy(z).wait_recv()
        total = from_x[z].astype(jnp.float32) + from_core[z, my_x].astype(jnp.float32)
        from_x[z] = total.astype(jnp.bfloat16)

        @pl.when(z != my_z)
        def _():
            z_copy(z, my_z).start()

        return 0

    tail = n_chunks - 1
    tail_rows = rows_of(tail)

    def hidden_part(at_rows, at):
        total = jnp.dot(gfull[0, at_rows, :], down_v[:d_own, at], preferred_element_type=jnp.float32)
        for g in range(1, n_rep):
            total += jnp.dot(gfull[g, at_rows, :], down_v[g * d_own:(g + 1) * d_own, at],
                             preferred_element_type=jnp.float32)
        passed = hid[at_rows, at].astype(jnp.float32) > 0.0
        masked[rep, at_rows, at] = jnp.where(passed, total, 0.0).astype(jnp.bfloat16)

    def grads_arrived(c):
        for o in offsets:
            grad_copy(c, o, behind(o)).wait_recv()

    def chunk(c, _):
        grads_arrived(c)

        def hidden_tile(j, _):
            hidden_part(rows_of(c), tile_at(j))
            for o in offsets:
                part_copy(c, j, o).start()
            return 0

        lax.fori_loop(0, n_tiles, hidden_tile, 0)
        return 0

    def tail_chunk():
        grads_arrived(tail)

        def hidden_piece(j, _):
            hidden_part(tail_rows, piece_at(j))
            for o in offsets:
                tail_copy(j, o).start()
            return 0

        lax.fori_loop(0, n_pieces, hidden_piece, 0)

    def own_part(c, _):
        def own_tile(j, _):
            at = pl.ds(pl.multiple_of(j * d_tile, d_tile), d_tile)
            own_sum[rows_of(c), at] = jnp.dot(masked[rep, rows_of(c), :], up_all[rep, :, at],
                                              preferred_element_type=jnp.float32)
            return 0

        lax.fori_loop(0, d_all // d_tile, own_tile, 0)
        return 0

    def spread_start():
        for o in offsets:
            landed(o, my_z, my_x)
            pl.when(above)(lambda: along_z(o, my_z, 1).start())
            pl.when(below)(lambda: along_z(o, my_z, -1).start())
            over_x(o, my_z).start()
            over_core(o, my_z, my_x).start()

    def both_sides(d, visit):
        pl.when(my_z >= d)(lambda: visit(my_z - d, above, 1))
        pl.when(my_z + d < n_z)(lambda: visit(my_z + d, below, -1))

    def spread_z(d, _):
        def visit(z, goes_on, step):
            for o in offsets:
                landed(o, z, my_x)
                pl.when(goes_on)(lambda: along_z(o, z, step).start())
                over_core(o, z, my_x).start()

        both_sides(d, visit)
        return 0

    def cross_x(d, _):
        def visit(z, goes_on, step):
            for o in offsets:
                over_x(o, z).start()

        both_sides(d, visit)
        return 0

    def pass_core(z):
        for o in offsets:
            landed(o, z, 1 - my_x)
            over_core(o, z, 1 - my_x).start()

    def spread_core(d, _):
        both_sides(d, lambda z, goes_on, step: pass_core(z))
        return 0

    def spread_sent(z, _):
        for o in offsets:
            pl.when((z <= my_z) & above)(lambda: along_z(o, z, 1).wait_send())
            pl.when((z >= my_z) & below)(lambda: along_z(o, z, -1).wait_send())
        return 0

    def finish(c, _):
        at_rows = rows_of(c)
        for o in offsets:
            all_of(masked.at[behind(o), at_rows], p_recv.at[c, o - 1])

        def out_tile(j, _):
            at = pl.ds(pl.multiple_of(j * d_tile, d_tile), d_tile)

            def term(g):
                return jnp.dot(masked[g, at_rows, :], up_all[g, :, at], preferred_element_type=jnp.float32)

            if n_rep == 2:
                total = own_sum[at_rows, at] + term(1 - rep)
            else:
                total = sum_terms(term)
            ig_out[at_rows, at] = total.astype(jnp.bfloat16)
            return 0

        lax.fori_loop(0, d_all // d_tile, out_tile, 0)
        return 0

    def sum_terms(term):
        total = term(0)
        for g in range(1, n_rep):
            total += term(g)
        return total

    def tail_term(g, j, at):
        return jnp.dot(masked[g, tail_rows, piece_at(j)], up_all[g, piece_at(j), at],
                       preferred_element_type=jnp.float32)

    def tail_tiles(visit):
        def one(i, _):
            visit(pl.ds(pl.multiple_of(i * d_tile, d_tile), d_tile))
            return 0

        lax.fori_loop(0, d_all // d_tile, one, 0)

    def tail_first(g, ref, rows_at):
        def visit(at):
            ref[rows_at, at] = tail_term(g, 0, at)

        tail_tiles(visit)

    def tail_add(g, j, ref, rows_at):
        def visit(at):
            ref[rows_at, at] += tail_term(g, j, at)

        tail_tiles(visit)

    def tail_last(g, j):
        def visit(at):
            other = tail_term(g, j, at)
            if n_pieces > 1:
                other = other_sum[:, at] + other
            ig_out[tail_rows, at] = (own_sum[tail_rows, at] + other).astype(jnp.bfloat16)

        tail_tiles(visit)

    def own_tail():
        tail_first(rep, own_sum, tail_rows)

        def step(j, _):
            tail_add(rep, j, own_sum, tail_rows)
            return 0

        lax.fori_loop(1, n_pieces, step, 0)

    def other_tail():
        everything = pl.ds(0, CHUNK)
        if n_pieces > 1:
            tail_arrived(0, 1)
            tail_first(1 - rep, other_sum, everything)

            def step(j, _):
                tail_arrived(j, 1)
                tail_add(1 - rep, j, other_sum, everything)
                return 0

            lax.fori_loop(1, n_pieces - 1, step, 0)
        tail_arrived(n_pieces - 1, 1)
        tail_last(1 - rep, n_pieces - 1)

    def finish_tail():
        for o in offsets:
            for j in range(n_pieces):
                tail_arrived(j, o)

        def visit(at):
            total = sum_terms(lambda g: jnp.dot(masked[g, tail_rows, :], up_all[g, :, at],
                                                preferred_element_type=jnp.float32))
            ig_out[tail_rows, at] = total.astype(jnp.bfloat16)

        tail_tiles(visit)

    first_late, last_late = z_own, n_z - (n_rep - 1)
    third = max(n_chunks // 3, 1)
    lax.fori_loop(0, z_own, make_terms, 0)
    lax.fori_loop(0, z_own, add_core, 0)
    loads[2].start()
    spread_start()
    loads[3].start()
    know_line()
    lax.fori_loop(1, 2, spread_z, 0)
    for part in range(z_own - 1):
        for o in offsets:
            early_copy(part, o, behind(o)).wait_recv()
    lax.fori_loop(first_late, last_late, make_terms, 0)
    lax.fori_loop(first_late, last_late, add_core, 0)
    lax.fori_loop(1, 2, cross_x, 0)
    lax.fori_loop(2, min(3, n_z), spread_z, 0)
    lax.fori_loop(0, 1, add_x, 0)
    loads[2].wait()
    lax.fori_loop(0, third, chunk, 0)
    lax.fori_loop(1, z_own, add_x, 0)
    lax.fori_loop(third, 2 * third, chunk, 0)
    pass_core(my_z)
    lax.fori_loop(2 * third, tail, chunk, 0)
    tail_chunk()
    lax.fori_loop(3, n_z, spread_z, 0)
    lax.fori_loop(last_late, n_z, make_terms, 0)
    lax.fori_loop(last_late, n_z, add_core, 0)
    lax.fori_loop(2, n_z, cross_x, 0)
    lax.fori_loop(first_late, last_late, add_x, 0)
    loads[3].wait()
    if n_rep == 2:
        lax.fori_loop(0, tail, own_part, 0)
        own_tail()
    lax.fori_loop(1, 2, spread_core, 0)
    lax.fori_loop(last_late, n_z, add_x, 0)
    lax.fori_loop(2, n_z, spread_core, 0)
    for o in offsets:
        all_of(up_all.at[behind(o), pl.ds(0, ff // 2)], uc_recv.at[o - 1])
    lax.fori_loop(0, tail, finish, 0)

    total = from_x[my_z].astype(jnp.float32)
    all_of(from_z, z_recv)
    for o in range(n_z - 1):
        total += from_z[o].astype(jnp.float32)
    dg_out[...] = total / n_dp

    for o in offsets:
        for part in range(z_own - 1):
            early_copy(part, o, rep).wait_send()
        all_of(grad.at[:, last_cols], g_send.at[o - 1])
        up_rep_copy(o).wait_send()
        all_of(up_all.at[behind(o), pl.ds(0, ff // 2)], uc_send.at[o - 1])
        all_of(up_all.at[behind(o), pl.ds(0, ff // 4)], ux_send.at[o - 1])
    lax.fori_loop(0, n_z, spread_sent, 0)
    all_of(from_core, c_send)
    all_of(from_x, x_send)
    all_of(from_z, z_send)

    if n_rep == 2:
        other_tail()
    else:
        finish_tail()
    for o in offsets:
        all_of(masked.at[rep], p_send.at[o - 1])


def store(n_parts, ig, dg, ig_out, dg_out, sem):
    part = ig.shape[0] // n_parts
    copies = [pltpu.make_async_copy(ig.at[pl.ds(i * part, part)], ig_out.at[pl.ds(i * part, part)], sem.at[i])
              for i in range(n_parts)]
    copies.append(pltpu.make_async_copy(dg, dg_out, sem.at[n_parts]))
    for copy in copies:
        copy.start()
    for copy in copies:
        copy.wait()


def on_device(n_dp, n_rep, grad_out, pre_act, up_weight, down_weight, slot_counts):
    rows, d_own = grad_out.shape
    ff = pre_act.shape[1]
    d_all = down_weight.shape[0]
    n_z = n_dp // 4
    blk = d_all // n_dp
    n_chunks = rows // CHUNK
    n_pieces = ff // piece_of(ff)
    z_own, others = n_z // n_rep, n_rep - 1
    any_ref = pl.BlockSpec(memory_space=pl.ANY)
    in_vmem = pl.BlockSpec(memory_space=pltpu.VMEM)
    bf16, dma = jnp.bfloat16, pltpu.SemaphoreType.DMA
    results = pl.pallas_call(
        functools.partial(kernel, n_dp, n_rep),
        out_shape=(pltpu.VMEM((rows, d_all), bf16), pltpu.VMEM((blk, ff), jnp.float32)),
        in_specs=[pl.BlockSpec(memory_space=pltpu.SMEM)] + [any_ref] * 4,
        out_specs=(in_vmem,) * 2,
        scratch_shapes=[
            pltpu.VMEM((n_rep, rows, d_own), bf16),
            pltpu.VMEM((rows, ff), bf16),
            pltpu.VMEM((n_rep, ff, d_all), bf16),
            pltpu.VMEM((d_all, ff), bf16),
            pltpu.VMEM((n_z, 2, 2, blk, ff), bf16),
            pltpu.VMEM((n_z, 2, blk, ff), bf16),
            pltpu.VMEM((n_z, blk, ff), bf16),
            pltpu.VMEM((n_z - 1, blk, ff), bf16),
            pltpu.VMEM((n_rep, rows, ff), bf16),
            pltpu.VMEM((rows, d_all), jnp.float32),
            pltpu.VMEM((CHUNK, d_all), jnp.float32),
            pltpu.SemaphoreType.REGULAR((2,)),
            dma((4,)), dma((max(z_own - 1, 1), others)), dma((max(z_own - 1, 1), others)),
            dma((others,)), dma((n_chunks, others)),
            dma((others,)), dma((n_chunks - 1, others)), dma((n_pieces, others)),
            dma((others,)), dma((n_z + 1, others)), dma((others,)), dma((others,)),
            dma((2 * n_z, others)), dma((others,)),
            dma, dma((n_z,)), dma, dma((n_z,)), dma, dma,
        ],
        compiler_params=pltpu.CompilerParams(
            collective_id=0, has_side_effects=True, vmem_limit_bytes=56 * 2**20),
    )(slot_counts, grad_out, pre_act, up_weight, down_weight)
    n_parts = 4
    return pl.pallas_call(
        functools.partial(store, n_parts),
        out_shape=(jax.ShapeDtypeStruct((rows, d_all), bf16), jax.ShapeDtypeStruct((blk, ff), jnp.float32)),
        in_specs=[in_vmem] * 2,
        out_specs=(any_ref,) * 2,
        scratch_shapes=[dma((n_parts + 1,))],
        compiler_params=pltpu.CompilerParams(vmem_limit_bytes=6 * 2**20),
    )(*results)


def solution(mesh):
    sizes = dict(mesh.shape)
    return jax.shard_map(
        functools.partial(on_device, sizes["dp"], sizes["rep"]),
        mesh=mesh,
        in_specs=(P("dp", "rep"), P("dp", "rep"), P("rep", None), P(None, "rep"), P("dp")),
        out_specs=(P("dp", None), P("dp", "rep")),
        check_vma=False,
    )
```

time: 120 us -> 104 us (0.87)
  the two profiles are of different devices: /device:TPU:28 before, /device:TPU:0 now
where the time goes in v2:
time: 104 us; the launch traced here: 103 us
  Pallas kernels  101 us (97%)
  between operations  1.29 us (1%)
    pallas_call x1, Pallas kernels, on_device(): pl.pallas_call(functools.partial(kernel, n_dp, n_rep), out_shape=(pltpu.V...  99.3 us

profile of v2, /device:TPU:0, one launch (start us, length us, event | category | flops | bytes accessed | tf_op | source)
XLA Modules:
  0.0 102.6 jit_solution(10001583886103144806)
XLA Ops:
  1.3 99.3 %shard_map.68 = (bf16[768,2048]{1,0:T(8,128)(2,1)S(1)}, f32[128,1536]{1,0:T(8,128)S(1)}) custom-call(s32[1]{0:T(128)S(6)} %copy.7.counts, bf16[768,1024]{1,0:T(8,128)(2,1)} %grad.1, bf16[768,1536]{1,0:T(8,128)(2,1)} %pre.1, bf16[1536,2048]{1,0:T(8,128)(2,1)} %up.1, bf16[2048,1536]{1,0:T(8,128)(2,1)} %down.1), custom_call_target="tpu_custom_call" | custom-call | tf_op jit(solution)/shard_map/pallas_call | solution.py:517
  100.6 2.0 %shard_map.69 = (bf16[768,2048]{1,0:T(8,128)(2,1)}, f32[128,1536]{1,0:T(8,128)}) custom-call(bf16[768,2048]{1,0:T(8,128)(2,1)S(1)} %get-tuple-element.4.ig, f32[128,1536]{1,0:T(8,128)S(1)} %get-tuple-element.5.dg), custom_call_target="tpu_custom_call" | custom-call | tf_op jit(solution)/shard_map/pallas_call | solution.py:546

commit v3 on v2

--- a/solution.py
+++ b/solution.py
@@ -79,8 +79,8 @@
         for i, (src, dst) in enumerate(
             ((grad, gfull.at[rep]), (pre, hid), (down, down_v), (up, up_all.at[rep])))
     ]
+    loads[0].start()
     loads[1].start()
-    loads[0].start()
     pl.semaphore_wait(barrier, len(near) + above.astype(jnp.int32) + below.astype(jnp.int32))
 
     def rows_of(c):
@@ -89,12 +89,12 @@
     last_cols = pl.ds((z_own - 1) * 4 * blk, 4 * blk)
 
     def grad_copy(c, o, source):
-        return send(grad.at[rows_of(c), last_cols], gfull.at[source, rows_of(c), last_cols],
+        return send(gfull.at[rep, rows_of(c), last_cols], gfull.at[source, rows_of(c), last_cols],
                     g_send.at[o - 1], g_recv.at[c, o - 1], {"rep": ahead(o)})
 
     def early_copy(part, o, source):
         cols = pl.ds(part * 4 * blk, 4 * blk)
-        return send(grad.at[:, cols], gfull.at[source, :, cols],
+        return send(gfull.at[rep, :, cols], gfull.at[source, :, cols],
                     gp_send.at[part, o - 1], gp_recv.at[part, o - 1], {"rep": ahead(o)})
 
     def tile_at(j):
@@ -148,6 +148,7 @@
 
     for o in offsets:
         up_rep_copy(o).start()
+    loads[0].wait()
     for part in range(z_own - 1):
         for o in offsets:
             early_copy(part, o, rep).start()
@@ -168,7 +169,6 @@
         return 0
 
     lax.fori_loop(0, n_chunks, mask_rows, 0)
-    loads[0].wait()
 
     def know_line():
         @pl.when(below)
@@ -362,11 +362,8 @@
                        preferred_element_type=jnp.float32)
 
     def tail_tiles(visit):
-        def one(i, _):
-            visit(pl.ds(pl.multiple_of(i * d_tile, d_tile), d_tile))
-            return 0
-
-        lax.fori_loop(0, d_all // d_tile, one, 0)
+        for i in range(d_all // d_tile):
+            visit(pl.ds(i * d_tile, d_tile))
 
     def tail_first(g, ref, rows_at):
         def visit(at):
@@ -398,18 +395,25 @@
 
         lax.fori_loop(1, n_pieces, step, 0)
 
-    def other_tail():
+    def other_tail(first, last):
         everything = pl.ds(0, CHUNK)
-        if n_pieces > 1:
-            tail_arrived(0, 1)
-            tail_first(1 - rep, other_sum, everything)
-
-            def step(j, _):
-                tail_arrived(j, 1)
+
+        def step(j, _):
+            tail_arrived(j, 1)
+
+            @pl.when(j == 0)
+            def _():
+                tail_first(1 - rep, other_sum, everything)
+
+            @pl.when(j > 0)
+            def _():
                 tail_add(1 - rep, j, other_sum, everything)
-                return 0
-
-            lax.fori_loop(1, n_pieces - 1, step, 0)
+
+            return 0
+
+        lax.fori_loop(first, last, step, 0)
+
+    def last_tail():
         tail_arrived(n_pieces - 1, 1)
         tail_last(1 - rep, n_pieces - 1)
 
@@ -438,53 +442,56 @@
         for o in offsets:
             early_copy(part, o, behind(o)).wait_recv()
     lax.fori_loop(first_late, last_late, make_terms, 0)
+    lax.fori_loop(2, min(3, n_z), spread_z, 0)
     lax.fori_loop(first_late, last_late, add_core, 0)
     lax.fori_loop(1, 2, cross_x, 0)
-    lax.fori_loop(2, min(3, n_z), spread_z, 0)
-    lax.fori_loop(0, 1, add_x, 0)
     loads[2].wait()
     lax.fori_loop(0, third, chunk, 0)
-    lax.fori_loop(1, z_own, add_x, 0)
     lax.fori_loop(third, 2 * third, chunk, 0)
+    lax.fori_loop(0, z_own, add_x, 0)
     pass_core(my_z)
     lax.fori_loop(2 * third, tail, chunk, 0)
     tail_chunk()
-    lax.fori_loop(3, n_z, spread_z, 0)
     lax.fori_loop(last_late, n_z, make_terms, 0)
     lax.fori_loop(last_late, n_z, add_core, 0)
-    lax.fori_loop(2, n_z, cross_x, 0)
+    lax.fori_loop(2, min(3, n_z), cross_x, 0)
     lax.fori_loop(first_late, last_late, add_x, 0)
+    lax.fori_loop(3, n_z, spread_z, 0)
+    lax.fori_loop(3, n_z, cross_x, 0)
     loads[3].wait()
     if n_rep == 2:
         lax.fori_loop(0, tail, own_part, 0)
         own_tail()
-    lax.fori_loop(1, 2, spread_core, 0)
     lax.fori_loop(last_late, n_z, add_x, 0)
-    lax.fori_loop(2, n_z, spread_core, 0)
+    lax.fori_loop(1, n_z, spread_core, 0)
     for o in offsets:
         all_of(up_all.at[behind(o), pl.ds(0, ff // 2)], uc_recv.at[o - 1])
     lax.fori_loop(0, tail, finish, 0)
 
-    total = from_x[my_z].astype(jnp.float32)
-    all_of(from_z, z_recv)
-    for o in range(n_z - 1):
-        total += from_z[o].astype(jnp.float32)
-    dg_out[...] = total / n_dp
-
     for o in offsets:
         for part in range(z_own - 1):
             early_copy(part, o, rep).wait_send()
-        all_of(grad.at[:, last_cols], g_send.at[o - 1])
+        all_of(gfull.at[rep, :, last_cols], g_send.at[o - 1])
         up_rep_copy(o).wait_send()
         all_of(up_all.at[behind(o), pl.ds(0, ff // 2)], uc_send.at[o - 1])
         all_of(up_all.at[behind(o), pl.ds(0, ff // 4)], ux_send.at[o - 1])
     lax.fori_loop(0, n_z, spread_sent, 0)
     all_of(from_core, c_send)
     all_of(from_x, x_send)
+
+    if n_rep == 2:
+        other_tail(0, n_pieces - 2)
+
+    total = from_x[my_z].astype(jnp.float32)
+    all_of(from_z, z_recv)
+    for o in range(n_z - 1):
+        total += from_z[o].astype(jnp.float32)
+    dg_out[...] = total / n_dp
     all_of(from_z, z_send)
 
     if n_rep == 2:
-        other_tail()
+        other_tail(max(n_pieces - 2, 0), n_pieces - 1)
+        last_tail()
     else:
         finish_tail()
     for o in offsets:

time: 104 us -> 102 us (0.981); the launches traced: 103 us -> 102 us
  no operation moved by 1% of the time
where the time goes in v3:
time: 102 us
  Pallas kernels  101 us (99%)
  between operations  1.29 us (1%)
    pallas_call x1, Pallas kernels, on_device(): pl.pallas_call(functools.partial(kernel, n_dp, n_rep), out_shape=(pltpu.V...  98.8 us

profile of v3, /device:TPU:0, one launch (start us, length us, event | category | flops | bytes accessed | tf_op | source)
XLA Modules:
  0.0 102.0 jit_solution(16271757105283016974)
XLA Ops:
  1.3 98.8 %shard_map.68 = (bf16[768,2048]{1,0:T(8,128)(2,1)S(1)}, f32[128,1536]{1,0:T(8,128)S(1)}) custom-call(s32[1]{0:T(128)S(6)} %copy.7.counts, bf16[768,1024]{1,0:T(8,128)(2,1)} %grad.1, bf16[768,1536]{1,0:T(8,128)(2,1)} %pre.1, bf16[1536,2048]{1,0:T(8,128)(2,1)} %up.1, bf16[2048,1536]{1,0:T(8,128)(2,1)} %down.1), custom_call_target="tpu_custom_call" | custom-call | tf_op jit(solution)/shard_map/pallas_call | solution.py:524
  100.1 2.0 %shard_map.69 = (bf16[768,2048]{1,0:T(8,128)(2,1)}, f32[128,1536]{1,0:T(8,128)}) custom-call(bf16[768,2048]{1,0:T(8,128)(2,1)S(1)} %get-tuple-element.4.ig, f32[128,1536]{1,0:T(8,128)S(1)} %get-tuple-element.5.dg), custom_call_target="tpu_custom_call" | custom-call | tf_op jit(solution)/shard_map/pallas_call | solution.py:553

commit v4 on v3

--- a/solution.py
+++ b/solution.py
@@ -21,7 +21,7 @@
 
 def kernel(n_dp, n_rep, counts, grad, pre, up, down, ig_out, dg_out,
            gfull, hid, up_all, down_v, terms, from_core, from_x, from_z, masked, own_sum, other_sum,
-           far_sem, load_sem, gp_send, gp_recv, g_send, g_recv, p_send, p_recv, t_recv, uy_send, uz_send, ux_send,
+           in_sem, load_sem, gp_send, gp_recv, g_send, g_recv, p_send, p_recv, t_recv, uy_send, uz_send, ux_send,
            uc_send, u_recv, uc_recv, c_send, c_recv, x_send, x_recv, z_send, z_recv):
     rows, d_own = grad.shape
     ff = pre.shape[1]
@@ -68,11 +68,11 @@
         pl.semaphore_signal(sem, inc=1, device_id=peer, device_id_type=MESH)
 
     barrier = pltpu.get_barrier_semaphore()
-    near = [{"rep": ahead(o)} for o in offsets] + [core_peer, x_peer]
-    for peer in near:
-        signal(barrier, peer)
+    for o in offsets:
+        signal(barrier, {"rep": ahead(o)})
+    pl.when(my_x == 0)(lambda: signal(barrier, x_peer))
+    pl.when(my_c == 0)(lambda: signal(barrier, core_peer))
     pl.when(above)(lambda: signal(barrier, z_peer(my_z + 1)))
-    pl.when(below)(lambda: signal(barrier, z_peer(my_z - 1)))
 
     loads = [
         pltpu.make_async_copy(src, dst, load_sem.at[i])
@@ -81,7 +81,7 @@
     ]
     loads[0].start()
     loads[1].start()
-    pl.semaphore_wait(barrier, len(near) + above.astype(jnp.int32) + below.astype(jnp.int32))
+    pl.semaphore_wait(barrier, n_rep - 1 + my_x + my_c + below.astype(jnp.int32))
 
     def rows_of(c):
         return pl.ds(pl.multiple_of(c * CHUNK, CHUNK), CHUNK)
@@ -155,8 +155,9 @@
     for c in range(n_chunks):
         for o in offsets:
             grad_copy(c, o, rep).start()
-    pl.when(my_z == 0)(lambda: signal(far_sem.at[0], z_peer(my_z + 1)))
-    pl.when(my_z == n_z - 1)(lambda: signal(far_sem.at[1], z_peer(my_z - 1)))
+    pl.when(my_c == 1)(lambda: signal(in_sem.at[0], core_peer))
+    pl.when(my_x == 1)(lambda: signal(in_sem.at[1], x_peer))
+    pl.when(my_z == n_z - 1)(lambda: signal(in_sem.at[2], z_peer(my_z - 1)))
 
     loads[1].wait()
     count = counts[0]
@@ -170,16 +171,21 @@
 
     lax.fori_loop(0, n_chunks, mask_rows, 0)
 
-    def know_line():
-        @pl.when(below)
-        def _():
-            pl.semaphore_wait(far_sem.at[0], 1)
-            pl.when(above)(lambda: signal(far_sem.at[0], z_peer(my_z + 1)))
-
+    def know_core():
+        pl.when(my_c == 0)(lambda: pl.semaphore_wait(in_sem.at[0], 1))
+
+    def know_x():
+        pl.when(my_x == 0)(lambda: pl.semaphore_wait(in_sem.at[1], 1))
+
+    def know_above():
         @pl.when(above)
         def _():
-            pl.semaphore_wait(far_sem.at[1], 1)
-            pl.when(below)(lambda: signal(far_sem.at[1], z_peer(my_z - 1)))
+            pl.semaphore_wait(in_sem.at[2], 1)
+            pl.when(below)(lambda: signal(in_sem.at[2], z_peer(my_z - 1)))
+
+    def know_below():
+        pl.when(below)(lambda: pl.semaphore_wait(in_sem.at[3], 1))
+        pl.when(above)(lambda: signal(in_sem.at[3], z_peer(my_z + 1)))
 
     def core_copy(z):
         return send(terms.at[z, 1 - my_c], from_core.at[z], c_send, c_recv.at[z], core_peer)
@@ -431,12 +437,15 @@
 
     first_late, last_late = z_own, n_z - (n_rep - 1)
     third = max(n_chunks // 3, 1)
+    know_core()
     lax.fori_loop(0, z_own, make_terms, 0)
+    know_x()
+    know_above()
     lax.fori_loop(0, z_own, add_core, 0)
     loads[2].start()
     spread_start()
     loads[3].start()
-    know_line()
+    know_below()
     lax.fori_loop(1, 2, spread_z, 0)
     for part in range(z_own - 1):
         for o in offsets:
@@ -538,7 +547,7 @@
             pltpu.VMEM((n_rep, rows, ff), bf16),
             pltpu.VMEM((rows, d_all), jnp.float32),
             pltpu.VMEM((CHUNK, d_all), jnp.float32),
-            pltpu.SemaphoreType.REGULAR((2,)),
+            pltpu.SemaphoreType.REGULAR((4,)),
             dma((4,)), dma((max(z_own - 1, 1), others)), dma((max(z_own - 1, 1), others)),
             dma((others,)), dma((n_chunks, others)),
             dma((others,)), dma((n_chunks - 1, others)), dma((n_pieces, others)),

time: 102 us -> 102 us (level)
  no operation moved by 1% of the time
where the time goes in v4:
time: 102 us; the launch traced here: 101 us
  Pallas kernels  100 us (98%)
  between operations  1.29 us (1%)
    pallas_call x1, Pallas kernels, on_device(): pl.pallas_call(functools.partial(kernel, n_dp, n_rep), out_shape=(pltpu.V...  98.2 us

profile of v4, /device:TPU:0, one launch (start us, length us, event | category | flops | bytes accessed | tf_op | source)
XLA Modules:
  0.0 101.4 jit_solution(7534073931204781223)
XLA Ops:
  1.3 98.2 %shard_map.68 = (bf16[768,2048]{1,0:T(8,128)(2,1)S(1)}, f32[128,1536]{1,0:T(8,128)S(1)}) custom-call(s32[1]{0:T(128)S(6)} %copy.7.counts, bf16[768,1024]{1,0:T(8,128)(2,1)} %grad.1, bf16[768,1536]{1,0:T(8,128)(2,1)} %pre.1, bf16[1536,2048]{1,0:T(8,128)(2,1)} %up.1, bf16[2048,1536]{1,0:T(8,128)(2,1)} %down.1), custom_call_target="tpu_custom_call" | custom-call | tf_op jit(solution)/shard_map/pallas_call | solution.py:533
  99.4 2.0 %shard_map.69 = (bf16[768,2048]{1,0:T(8,128)(2,1)}, f32[128,1536]{1,0:T(8,128)}) custom-call(bf16[768,2048]{1,0:T(8,128)(2,1)S(1)} %get-tuple-element.4.ig, f32[128,1536]{1,0:T(8,128)S(1)} %get-tuple-element.5.dg), custom_call_target="tpu_custom_call" | custom-call | tf_op jit(solution)/shard_map/pallas_call | solution.py:562
